TPU v7x, 32 devices: a whole 2x2x4 slice. The times are simulated.
32 devices in a mesh: ctx: 8 (over y, x, core), head: 4 (over z).
Axes of the slice: x: 2, y: 2, z: 4, core: 2. Of those that a mesh axis runs over, the one named last changes fastest.
Arguments:
- block_order: int32 [16], replicated, may hold values from 0 to 15, as said below
- query_latent: bfloat16 [1024, 128, 576], P('ctx', 'head'), may hold values from -12 to 12
- key_latent: bfloat16 [1024, 576], P('ctx'), may hold values from -6 to 6
- normalizer: float32 [1024, 128], P('ctx', 'head'), may hold values from 6 to 9
- indexer_query: bfloat16 [1024, 64, 128], P('ctx', 'head'), may hold values from -8 to 8
- indexer_key: bfloat16 [1024, 128], P('ctx'), may hold values from -4 to 4
- indexer_weight: bfloat16 [1024, 64], P('ctx', 'head'), may hold values from -4 to 4
Outputs:
- query_grad: float32 [1024, 64, 128], P('ctx', 'head')
- key_grad: float32 [1024, 128], P(('ctx', 'head'))
Inputs may be any that keep to these rules, and one draw needn't show every extreme that they name: `block_order`: entries 2 i and 2 i + 1 are the blocks stored on ctx index i; all entries together are each of 0 to 15 once, and the two entries of one index sum to 15.
All inputs are finite; a program needn't handle non-finite values.
Results may differ from a plain program's by a relative error of at most 0.0037.
Values may be sent and summed in bfloat16 or wider, within the bound.
A program may use at most 128 MiB of HBM per device.

v0:
```python
import math
import jax
import jax.numpy as jnp
from jax import lax
from jax.sharding import PartitionSpec as P

mla_scale = 192.0 ** (-0.5)
loss_scale = 64.0


def gradient(tile_sums, query_pos, key_pos):
    visible = key_pos[None, :] <= query_pos[:, None]
    target_sum = jnp.where(visible, tile_sums[0], 0.0)
    row_total = jnp.sum(target_sum, axis=1, keepdims=True)
    logits = tile_sums[1]
    row_top = jnp.max(jnp.where(visible, logits, -jnp.inf), axis=1, keepdims=True)
    exp_logit = jnp.where(visible, jnp.exp(logits - row_top), 0.0)
    norm_sum = jnp.sum(exp_logit, axis=1, keepdims=True)
    return jnp.where(
        visible, loss_scale * (exp_logit / norm_sum - target_sum / row_total), 0.0
    ).astype(jnp.bfloat16)


def per_device(
    block_order, query_latent, key_latent, normalizer, indexer_query, indexer_key, indexer_weight
):
    query_rows = query_latent.shape[0]
    block_rows = query_rows // 2
    cycle_count = lax.axis_size("ctx")
    group_count = lax.axis_size("head")
    tokens = query_rows * cycle_count
    local_heads = indexer_query.shape[1]
    idx_scale = (local_heads * group_count * indexer_query.shape[2]) ** (-0.5)
    key_pos = (
        block_order[:, None] * block_rows + jnp.arange(block_rows, dtype=jnp.int32)[None, :]
    ).reshape(-1)
    query_pos = lax.dynamic_slice_in_dim(key_pos, lax.axis_index("ctx") * query_rows, query_rows, 0)
    all_latent, all_index = (
        lax.all_gather(key_latent, "ctx", axis=0, tiled=True),
        lax.all_gather(indexer_key, "ctx", axis=0, tiled=True),
    )
    key_block = math.gcd(tokens, 512)
    block_count = tokens // key_block
    weight_float = indexer_weight.astype(jnp.float32)

    def forward(step_index, state):
        tile_sums, positive = state
        offset = step_index * key_block
        latent_block = lax.dynamic_slice_in_dim(all_latent, offset, key_block, 0)
        index_block = lax.dynamic_slice_in_dim(all_index, offset, key_block, 0)
        scores = (
            jnp.einsum(
                "thl,sl->ths", query_latent, latent_block, preferred_element_type=jnp.float32
            )
            * mla_scale
        )
        target_part = jnp.sum(jnp.exp(scores - normalizer[:, :, None]), axis=1)
        idx_dot = jnp.einsum(
            "tjd,sd->tjs", indexer_query, index_block, preferred_element_type=jnp.float32
        )
        logit_part = idx_scale * jnp.sum(
            weight_float[:, :, None] * jnp.maximum(idx_dot, 0.0), axis=1
        )
        tile_sums = lax.dynamic_update_slice_in_dim(
            tile_sums, jnp.stack((target_part, logit_part)), offset, 2
        )
        positive = lax.dynamic_update_slice_in_dim(positive, idx_dot > 0, offset, 2)
        return (tile_sums, positive)

    start_state = (
        jnp.zeros((2, query_rows, tokens), jnp.float32),
        jnp.zeros((query_rows, local_heads, tokens), jnp.bool_),
    )
    tile_sums, positive = lax.fori_loop(0, block_count, forward, start_state)
    share_sums = lax.psum_scatter(tile_sums, "head", scatter_dimension=1, tiled=True)
    share_count = query_rows // group_count
    share_pos = lax.dynamic_slice_in_dim(
        query_pos, lax.axis_index("head") * share_count, share_count, 0
    )
    share_grad = gradient(share_sums, share_pos, key_pos)
    grad_logit = lax.all_gather(share_grad, "head", axis=0, tiled=True)
    weight_scaled = weight_float * idx_scale

    def backward(step_index, state):
        coeff_buffer, query_accum = state
        offset = step_index * key_block
        positive_block = lax.dynamic_slice_in_dim(positive, offset, key_block, 2)
        grad_block = lax.dynamic_slice_in_dim(grad_logit, offset, key_block, 1)
        coeff_block = jnp.where(
            positive_block,
            grad_block.astype(jnp.float32)[:, None, :] * weight_scaled[:, :, None],
            0.0,
        ).astype(jnp.bfloat16)
        index_block = lax.dynamic_slice_in_dim(all_index, offset, key_block, 0)
        query_accum = query_accum + jnp.einsum(
            "tjs,sd->tjd", coeff_block, index_block, preferred_element_type=jnp.float32
        )
        coeff_buffer = lax.dynamic_update_slice_in_dim(coeff_buffer, coeff_block, offset, 2)
        return (coeff_buffer, query_accum)

    back_state = (
        jnp.zeros((query_rows, local_heads, tokens), jnp.bfloat16),
        jnp.zeros(indexer_query.shape, jnp.float32),
    )
    coefficient, query_grad = lax.fori_loop(0, block_count, backward, back_state)
    key_grad = lax.psum_scatter(
        jnp.einsum("tjs,tjd->sd", coefficient, indexer_query, preferred_element_type=jnp.float32),
        ("ctx", "head"),
        scatter_dimension=0,
        tiled=True,
    )
    return (query_grad, key_grad)


def solution(mesh):
    return jax.shard_map(
        per_device,
        mesh=mesh,
        in_specs=(
            P(),
            P("ctx", "head", None),
            P("ctx", None),
            P("ctx", "head"),
            P("ctx", "head", None),
            P("ctx", None),
            P("ctx", "head"),
        ),
        out_specs=(P("ctx", "head", None), P(("ctx", "head"), None)),
        check_vma=False,
    )
```

profile of v0, /device:TPU:0, one launch (start us, length us, event | category | flops | bytes accessed | tf_op | source)
XLA Modules:
  0.0 269.6 jit_solution(7283531578134878488)
XLA Ops:
  7.2 0.7 all-gather.2.cloned.1.call-update
  8.0 0.7 convert_element_type.20
  8.6 1.2 copy.14
  9.8 11.0 %all_gather.10 = bf16[1024,128]{1,0:T(8,128)(2,1)S(1)} all-gather(bf16[128,128]{1,0:T(8,128)(2,1)} %param.16), channel_id=1, replica_groups=mesh['ctx'=8,'head'=4] {'ctx'}, dimensions={0}, use_global_device_ids=true | all-gather | bytes 294912 | tf_op jit(solution)/shard_map/all_gather | solution.py:40
  20.8 15.8 %all-gather.2.cloned.1.call-done = bf16[1024,576]{0,1:T(8,128)(2,1)} async-done(((bf16[128,576]{0,1:T(8,128)(2,1)}), bf16[1024,576]{0,1:T(8,128)(2,1)}) %all-gather.2.cloned.1.call-update) | async-done | bytes 1179664 | tf_op jit(solution)/shard_map/all_gather | solution.py:39
  36.7 1.1 broadcast_in_dim.49.clone
  37.8 0.8 broadcast_in_dim.50
  38.6 27.1 %while.31 = (s32[]{:T(128)}, f32[2,128,1024]{2,1,0:T(8,128)}, pred[128,16,1024]{0,2,1:T(32,128)(4,1)S(1)}, bf16[1024,576]{0,1:T(8,128)(2,1)}, bf16[128,32,576]{0...) while((s32[]{:T(128)}, f32[2,128,1024]{2,1,0:T(8,128)}, ...), condition=%wide.region_3.0_spmd, body=%wide.region_0.0_spmd.sunk | while | flops 2694905856 | bytes 23814388 | solution.py:74
  38.7 6.8 %exponential_reduce_fusion.2 = f32[512,128]{1,0:T(8,128)S(1)} fusion(f32[128,32]{0,1:T(8,128)S(1)} %get-tuple-element.515, bf16[128,32,576]{0,2,1:T(8,128)(2,1)} %get-tuple-element.514, bf16[1024,576]{0,1:T(8,128)(2,1)} %get-tuple-element.513, s32[]{:T(128)S(6)} %select_n.87), kind=kOutput, calls=%fused_computation.clone.1 | convolution fusion | flops 2422145024 | bytes 5586948 | tf_op jit(solution)/shard_map/while/body/eval_jaxpr/thl,sl->ths/dot_general | solution.py:52
  45.5 2.7 multiply_reduce_fusion.2
  48.2 0.1 pad_maximum_fusion.2
  48.2 0.2 copy.30
  48.4 0.9 constant_dynamic-update-slice_fusion.2
  49.3 2.8 %bitcast_dynamic-update-slice_fusion.2 = pred[128,16,1024]{0,2,1:T(32,128)(4,1)S(1)} fusion(pred[128,16,1024]{0,2,1:T(32,128)(4,1)S(1)} %get-tuple-element.499, s32[]{:T(128)S(6)} %select_n.87, f32[512,128,16]{1,0,2:T(8,128)} %get-tuple-element.476), kind=kLoop, calls=%fused_computation.2.clone.1 | loop fusion | flops 1048576 | bytes 5242884 | tf_op jit(solution)/shard_map/while/body/eval_jaxpr/dynamic_update_slice | solution.py:67
  52.2 6.8 %exponential_reduce_fusion.2 = f32[512,128]{1,0:T(8,128)S(1)} fusion(f32[128,32]{0,1:T(8,128)S(1)} %get-tuple-element.515, bf16[128,32,576]{0,2,1:T(8,128)(2,1)} %get-tuple-element.514, bf16[1024,576]{0,1:T(8,128)(2,1)} %get-tuple-element.513, s32[]{:T(128)S(6)} %select_n.87), kind=kOutput, calls=%fused_computation.clone.1 | convolution fusion | flops 2422145024 | bytes 5586948 | tf_op jit(solution)/shard_map/while/body/eval_jaxpr/thl,sl->ths/dot_general | solution.py:52
  59.0 2.7 multiply_reduce_fusion.2
  61.7 0.1 pad_maximum_fusion.2
  61.8 0.2 copy.30
  62.0 0.9 constant_dynamic-update-slice_fusion.2
  62.9 2.8 %bitcast_dynamic-update-slice_fusion.2 = pred[128,16,1024]{0,2,1:T(32,128)(4,1)S(1)} fusion(pred[128,16,1024]{0,2,1:T(32,128)(4,1)S(1)} %get-tuple-element.499, s32[]{:T(128)S(6)} %select_n.87, f32[512,128,16]{1,0,2:T(8,128)} %get-tuple-element.476), kind=kLoop, calls=%fused_computation.2.clone.1 | loop fusion | flops 1048576 | bytes 5242884 | tf_op jit(solution)/shard_map/while/body/eval_jaxpr/dynamic_update_slice | solution.py:67
  65.8 0.0 reduce-scatter.5.cloned.1.call-start
  65.8 0.1 iota_add_fusion
  65.9 0.1 add.94
  66.0 0.1 dynamic_slice.42
  66.1 27.1 %reduce-scatter.3.cloned.1.call-done = f32[2,32,1024]{2,1,0:T(8,128)} async-done(((f32[2,128,1024]{2,1,0:T(8,128)}), f32[2,32,1024]{2,1,0:T(8,128)}) %reduce-scatter.3.cloned.1.call-update) | async-done | bytes 262160 | tf_op jit(solution)/shard_map/reduce_scatter | solution.py:75
  93.2 1.1 fusion.17
  94.3 1.2 fusion.20
  95.5 1.1 fusion.18
  96.6 14.5 %all_gather.11 = bf16[128,1024]{1,0:T(8,128)(2,1)S(1)} all-gather(bf16[32,1024]{1,0:T(8,128)(2,1)S(1)} %fusion.18), channel_id=1, replica_groups=mesh['ctx'=8,'head'=4] {'head'}, dimensions={0}, use_global_device_ids=true | all-gather | bytes 327680 | tf_op jit(solution)/shard_map/all_gather | solution.py:81
  111.0 2.5 broadcast_in_dim.47
  113.5 10.9 %while.32 = (s32[]{:T(128)}, bf16[128,16,1024]{2,0,1:T(8,128)(2,1)}, f32[128,16,128]{2,0,1:T(8,128)}, pred[128,16,1024]{0,2,1:T(32,128)(4,1)S(1)}, bf16[128,1024...) while((s32[]{:T(128)}, ...), condition=%wide.region_9.10_spmd.clone, body=%wide.region_8.9_spmd.clone.sunk | while | flops 275316736 | bytes 53494056 | solution.py:105
  113.6 0.1 constant_dynamic-slice_fusion.2
  113.6 1.2 copy.31
  114.9 1.0 fusion.36
  115.9 0.2 copy-done.2
  116.1 0.7 fusion.35
  116.8 0.3 copy-done.5
  117.1 1.9 copy-done.3
  119.0 0.1 constant_dynamic-slice_fusion.2
  119.1 1.2 copy.31
  120.4 1.0 fusion.36
  121.4 0.1 copy-done.2
  121.5 0.7 fusion.35
  122.2 0.3 copy-done.5
  122.5 1.9 copy-done.3
  124.4 4.4 %convolution_bitcast_fusion = f32[1024,128]{1,0:T(8,128)} fusion(bf16[128,16,1024]{2,0,1:T(8,128)(2,1)} %get-tuple-element.285, bf16[128,16,128]{2,1,0:T(8,128)(2,1)S(1)} %copy-done.7), kind=kOutput, calls=%fused_computation.26 | convolution fusion | flops 536870912 | bytes 5242880 | tf_op jit(solution)/shard_map/tjs,tjd->sd/dot_general | solution.py:107
  128.8 1.6 copy.19
  130.4 132.7 %reduce-scatter.5.cloned.1.call-done = f32[32,128]{1,0:T(8,128)} async-done(((f32[1024,128]{1,0:T(8,128)}), f32[32,128]{1,0:T(8,128)}) %reduce-scatter.5.cloned.1.call-update) | async-done | bytes 16400 | tf_op jit(solution)/shard_map/reduce_scatter | solution.py:106
  (39 shorter events, 0.3 us)
Async XLA Ops:
  7.2 31.4 %copy-start.9 = (f32[128,32]{0,1:T(8,128)S(1)}, f32[128,32]{0,1:T(8,128)}, u32[]{:S(2)}) copy-start(f32[128,32]{0,1:T(8,128)} %param.14) | copy-start | bytes 49156
  7.2 29.5 %all-gather.2.cloned.1.call-start = ((), (), s32[]{:S(2)}) async-start(), calls=%async_computation.2 | async-start | bytes 1327104 | tf_op jit(solution)/shard_map/all_gather | solution.py:39
  7.9 85.3 %reduce-scatter.3.cloned.1.call-start = ((), (), s32[]{:S(2)}) async-start(), calls=%async_computation.3 | async-start | bytes 1310720 | tf_op jit(solution)/shard_map/reduce_scatter | solution.py:75
  38.6 27.2 %copy-start.10 = (s32[16]{0:T(128)S(1)}, s32[16]{0:T(128)}, u32[]{:S(2)}) copy-start(s32[16]{0:T(128)} %param.11) | copy-start | bytes 196
  38.6 27.5 %copy-start.8 = (bf16[128,16]{0,1:T(8,128)(2,1)S(1)}, bf16[128,16]{0,1:T(8,128)(2,1)}, u32[]{:S(2)}) copy-start(bf16[128,16]{0,1:T(8,128)(2,1)} %param.17) | copy-start | bytes 12292
  38.6 6.8 %copy-start = (bf16[128,16,128]{2,0,1:T(8,128)(2,1)}, bf16[128,16,128]{2,0,1:T(8,128)(2,1)S(1)}, u32[]{:S(2)}) copy-start(bf16[128,16,128]{2,0,1:T(8,128)(2,1)S(1)} %get-tuple-element.518) | copy-start | bytes 1572868 | tf_op jit(solution)/shard_map/while
  48.4 3.7 %copy-start.1 = (bf16[128,16,128]{2,0,1:T(8,128)(2,1)S(1)}, bf16[128,16,128]{2,0,1:T(8,128)(2,1)}, u32[]{:S(2)}) copy-start(bf16[128,16,128]{2,0,1:T(8,128)(2,1)} %copy-done) | copy-start | bytes 1572868 | tf_op jit(solution)/shard_map/while
  52.2 6.8 %copy-start = (bf16[128,16,128]{2,0,1:T(8,128)(2,1)}, bf16[128,16,128]{2,0,1:T(8,128)(2,1)S(1)}, u32[]{:S(2)}) copy-start(bf16[128,16,128]{2,0,1:T(8,128)(2,1)S(1)} %get-tuple-element.518) | copy-start | bytes 1572868 | tf_op jit(solution)/shard_map/while
  62.0 3.7 %copy-start.1 = (bf16[128,16,128]{2,0,1:T(8,128)(2,1)S(1)}, bf16[128,16,128]{2,0,1:T(8,128)(2,1)}, u32[]{:S(2)}) copy-start(bf16[128,16,128]{2,0,1:T(8,128)(2,1)} %copy-done) | copy-start | bytes 1572868 | tf_op jit(solution)/shard_map/while
  65.8 197.3 %reduce-scatter.5.cloned.1.call-start = ((), (), s32[]{:S(2)}) async-start(), calls=%async_computation.4 | async-start | bytes 540672 | tf_op jit(solution)/shard_map/reduce_scatter | solution.py:106
  113.5 10.9 %copy-start.7 = (bf16[128,16,128]{2,1,0:T(8,128)(2,1)S(1)}, bf16[128,16,128]{2,1,0:T(8,128)(2,1)}, u32[]{:S(2)}) copy-start(bf16[128,16,128]{2,1,0:T(8,128)(2,1)} %param.15) | copy-start | bytes 1572868
  113.5 1.3 copy-start.4
  113.6 2.5 copy-start.2
  116.1 1.0 copy-start.5
  117.1 1.9 copy-start.3
  119.0 1.3 copy-start.4
  119.0 2.5 copy-start.2
  121.5 1.0 copy-start.5
  122.5 1.9 copy-start.3
  124.4 4.4 %copy-start.6 = (f32[128,16,128]{2,0,1:T(8,128)S(1)}, f32[128,16,128]{2,0,1:T(8,128)}, u32[]{:S(2)}) copy-start(f32[128,16,128]{2,0,1:T(8,128)} %get-tuple-element.344) | copy-start | bytes 3145732
Sparse Core Ops, SparseCore 0:
  9.9 26.7 all-gather.1
  65.9 27.2 reduce-scatter.2
  128.9 134.0 reduce-scatter.4
where the time goes:
time: 270 us
  waiting for transfers between devices  176 us (65%)
  blocking collectives  25.5 us (9%)
  matrix products  25.3 us (9%)
  local copies, waits for them, and re-layouts  16.9 us (6%)
  between operations  13.8 us (5%)
  other arithmetic  11.4 us (4%)
    reduce_scatter x1, waiting for transfers between devices, per_device(): lax.psum_scatter(jnp.einsum('tjs,tjd->sd', coefficient, indexer_query, pr...  133 us
    reduce_scatter x1, waiting for transfers between devices, per_device(): lax.psum_scatter(tile_sums, 'head', scatter_dimension=1, tiled=True)  27.1 us
    all_gather x1, waiting for transfers between devices, per_device(): lax.all_gather(key_latent, 'ctx', axis=0, tiled=True)  15.8 us
    all_gather x1, blocking collectives, per_device(): grad_logit = lax.all_gather(share_grad, 'head', axis=0, tiled=True)  14.5 us
    dot_general x2, matrix products, forward(): jnp.einsum('thl,sl->ths', query_latent, latent_block, preferred_element_t...  13.6 us
    all_gather x1, blocking collectives, per_device(): lax.all_gather(indexer_key, 'ctx', axis=0, tiled=True)  11 us
    dynamic_update_slice x2, other arithmetic, forward(): positive = lax.dynamic_update_slice_in_dim(positive, idx_dot > 0, offset, 2)  5.67 us
  transfers between devices with their start and end apart: 3, of which 3 were waited for; matrix products, arithmetic and copies ran while one was open for 1% of the time, Pallas kernels for 0%

commit v1 on v0

--- a/solution.py
+++ b/solution.py
@@ -6,6 +6,16 @@
 
 mla_scale = 192.0 ** (-0.5)
 loss_scale = 64.0
+
+
+def collect(x, axis, dim):
+    ways, here, turn = (lax.axis_size(axis), lax.axis_index(axis), x.shape[dim])
+    shape = [n * ways if d == dim else n for d, n in enumerate(x.shape)]
+    full = lax.dynamic_update_slice_in_dim(jnp.zeros(shape, x.dtype), x, here * turn, axis=dim)
+    for far in range(1, ways):
+        x = lax.ppermute(x, axis, [(d, (d + 1) % ways) for d in range(ways)])
+        full = lax.dynamic_update_slice_in_dim(full, x, (here - far) % ways * turn, axis=dim)
+    return full
 
 
 def gradient(tile_sums, query_pos, key_pos):
@@ -78,7 +88,7 @@
         query_pos, lax.axis_index("head") * share_count, share_count, 0
     )
     share_grad = gradient(share_sums, share_pos, key_pos)
-    grad_logit = lax.all_gather(share_grad, "head", axis=0, tiled=True)
+    grad_logit = collect(share_grad, "head", 0)
     weight_scaled = weight_float * idx_scale
 
     def backward(step_index, state):

time: 270 us -> 274 us (1.015)
  waiting for transfers between devices: 176 us -> 195 us
  blocking collectives: 25.5 us -> 11 us
    ppermute x0 -> x3, waiting for transfers between devices: none -> 18 us  [collect(): x = lax.ppermute(x, axis, [(d, (d + 1) % ways) for d in range(ways)])]
    all_gather x1 -> x0, blocking collectives: 14.5 us -> none  [per_device(): grad_logit = lax.all_gather(share_grad, 'head', axis=0, tiled=True)]
  transfers between devices with their start and end apart: 3 -> 6, of which waited for: 3 -> 6; matrix products, arithmetic and copies ran while one was open for 1% -> 1% of each run, Pallas kernels for 0% -> 0%
where the time goes in v1:
time: 274 us
  waiting for transfers between devices  195 us (71%)
  matrix products  25.3 us (9%)
  local copies, waits for them, and re-layouts  16.8 us (6%)
  between operations  14 us (5%)
  other arithmetic  11.4 us (4%)
  blocking collectives  11 us (4%)
    reduce_scatter x1, waiting for transfers between devices, per_device(): lax.psum_scatter(jnp.einsum('tjs,tjd->sd', coefficient, indexer_query, pr...  133 us
    reduce_scatter x1, waiting for transfers between devices, per_device(): lax.psum_scatter(tile_sums, 'head', scatter_dimension=1, tiled=True)  27.1 us
    ppermute x3, waiting for transfers between devices, collect(): x = lax.ppermute(x, axis, [(d, (d + 1) % ways) for d in range(ways)])  18 us
    all_gather x1, waiting for transfers between devices, per_device(): lax.all_gather(key_latent, 'ctx', axis=0, tiled=True)  15.8 us
    dot_general x2, matrix products, forward(): jnp.einsum('thl,sl->ths', query_latent, latent_block, preferred_element_t...  13.6 us
    all_gather x1, blocking collectives, per_device(): lax.all_gather(indexer_key, 'ctx', axis=0, tiled=True)  11 us
    dynamic_update_slice x2, other arithmetic, forward(): positive = lax.dynamic_update_slice_in_dim(positive, idx_dot > 0, offset, 2)  5.67 us
  transfers between devices with their start and end apart: 6, of which 6 were waited for; matrix products, arithmetic and copies ran while one was open for 1% of the time, Pallas kernels for 0%

profile of v1, /device:TPU:0, one launch (start us, length us, event | category | flops | bytes accessed | tf_op | source)
XLA Modules:
  0.0 273.6 jit_solution(5447429482198100509)
XLA Ops:
  7.2 0.7 all-gather.2.cloned.1.call-update
  8.0 0.7 convert_element_type.20
  8.6 1.2 copy.14
  9.8 11.0 %all_gather.7 = bf16[1024,128]{1,0:T(8,128)(2,1)S(1)} all-gather(bf16[128,128]{1,0:T(8,128)(2,1)} %param.16), channel_id=1, replica_groups=mesh['ctx'=8,'head'=4] {'ctx'}, dimensions={0}, use_global_device_ids=true | all-gather | bytes 294912 | tf_op jit(solution)/shard_map/all_gather | solution.py:50
  20.8 15.8 %all-gather.2.cloned.1.call-done = bf16[1024,576]{0,1:T(8,128)(2,1)} async-done(((bf16[128,576]{0,1:T(8,128)(2,1)}), bf16[1024,576]{0,1:T(8,128)(2,1)}) %all-gather.2.cloned.1.call-update) | async-done | bytes 1179664 | tf_op jit(solution)/shard_map/all_gather | solution.py:49
  36.7 1.1 broadcast_in_dim.52.clone
  37.8 0.8 broadcast_in_dim.53
  38.6 27.0 %while.31 = (s32[]{:T(128)}, f32[2,128,1024]{2,1,0:T(8,128)}, pred[128,16,1024]{0,2,1:T(32,128)(4,1)S(1)}, bf16[1024,576]{0,1:T(8,128)(2,1)}, bf16[128,32,576]{0...) while((s32[]{:T(128)}, f32[2,128,1024]{2,1,0:T(8,128)}, ...), condition=%wide.region_3.0_spmd, body=%wide.region_0.0_spmd.sunk | while | flops 2694905856 | bytes 23814388 | solution.py:84
  38.6 6.8 %exponential_reduce_fusion.2 = f32[512,128]{1,0:T(8,128)S(1)} fusion(f32[128,32]{0,1:T(8,128)S(1)} %get-tuple-element.517, bf16[128,32,576]{0,2,1:T(8,128)(2,1)} %get-tuple-element.516, bf16[1024,576]{0,1:T(8,128)(2,1)} %get-tuple-element.515, s32[]{:T(128)S(6)} %select_n.121), kind=kOutput, calls=%fused_computation.clone.1 | convolution fusion | flops 2422145024 | bytes 5586948 | tf_op jit(solution)/shard_map/while/body/eval_jaxpr/thl,sl->ths/dot_general | solution.py:62
  45.4 2.7 multiply_reduce_fusion.2
  48.1 0.1 pad_maximum_fusion.2
  48.2 0.2 copy.30
  48.4 0.8 constant_dynamic-update-slice_fusion.6
  49.2 2.8 %bitcast_dynamic-update-slice_fusion.2 = pred[128,16,1024]{0,2,1:T(32,128)(4,1)S(1)} fusion(pred[128,16,1024]{0,2,1:T(32,128)(4,1)S(1)} %get-tuple-element.501, s32[]{:T(128)S(6)} %select_n.121, f32[512,128,16]{1,0,2:T(8,128)} %get-tuple-element.478), kind=kLoop, calls=%fused_computation.2.clone.1 | loop fusion | flops 1048576 | bytes 5242884 | tf_op jit(solution)/shard_map/while/body/eval_jaxpr/dynamic_update_slice | solution.py:77
  52.1 6.8 %exponential_reduce_fusion.2 = f32[512,128]{1,0:T(8,128)S(1)} fusion(f32[128,32]{0,1:T(8,128)S(1)} %get-tuple-element.517, bf16[128,32,576]{0,2,1:T(8,128)(2,1)} %get-tuple-element.516, bf16[1024,576]{0,1:T(8,128)(2,1)} %get-tuple-element.515, s32[]{:T(128)S(6)} %select_n.121), kind=kOutput, calls=%fused_computation.clone.1 | convolution fusion | flops 2422145024 | bytes 5586948 | tf_op jit(solution)/shard_map/while/body/eval_jaxpr/thl,sl->ths/dot_general | solution.py:62
  58.9 2.7 multiply_reduce_fusion.2
  61.7 0.2 copy.30
  61.9 0.8 constant_dynamic-update-slice_fusion.6
  62.7 2.8 %bitcast_dynamic-update-slice_fusion.2 = pred[128,16,1024]{0,2,1:T(32,128)(4,1)S(1)} fusion(pred[128,16,1024]{0,2,1:T(32,128)(4,1)S(1)} %get-tuple-element.501, s32[]{:T(128)S(6)} %select_n.121, f32[512,128,16]{1,0,2:T(8,128)} %get-tuple-element.478), kind=kLoop, calls=%fused_computation.2.clone.1 | loop fusion | flops 1048576 | bytes 5242884 | tf_op jit(solution)/shard_map/while/body/eval_jaxpr/dynamic_update_slice | solution.py:77
  65.7 0.1 iota_add_fusion
  65.8 0.1 add.117
  65.9 0.1 dynamic_slice.42
  65.9 27.1 %reduce-scatter.3.cloned.1.call-done = f32[2,32,1024]{2,1,0:T(8,128)} async-done(((f32[2,128,1024]{2,1,0:T(8,128)}), f32[2,32,1024]{2,1,0:T(8,128)}) %reduce-scatter.3.cloned.1.call-update) | async-done | bytes 262160 | tf_op jit(solution)/shard_map/reduce_scatter | solution.py:85
  93.1 1.1 fusion.17
  94.2 1.2 fusion.20
  95.4 1.1 constant_dynamic-update-slice_fusion.4
  96.7 5.9 %collective-permute-done = bf16[32,1024]{1,0:T(8,128)(2,1)S(1)} collective-permute-done((bf16[32,1024]{1,0:T(8,128)(2,1)S(1)}, bf16[32,1024]{1,0:T(8,128)(2,1)S(1)}, u32[]{:S(2)}, u32[]{:S(2)}) %collective-permute-start) | collective-permute-done | bytes 65568 | tf_op jit(solution)/shard_map/ppermute | solution.py:16
  102.6 6.0 %collective-permute-done.1 = bf16[32,1024]{1,0:T(8,128)(2,1)S(1)} collective-permute-done((bf16[32,1024]{1,0:T(8,128)(2,1)S(1)}, bf16[32,1024]{1,0:T(8,128)(2,1)S(1)}, u32[]{:S(2)}, u32[]{:S(2)}) %collective-permute-start.1) | collective-permute-done | bytes 65568 | tf_op jit(solution)/shard_map/ppermute | solution.py:16
  108.7 6.0 %collective-permute-done.2 = bf16[32,1024]{1,0:T(8,128)(2,1)S(1)} collective-permute-done((bf16[32,1024]{1,0:T(8,128)(2,1)S(1)}, bf16[32,1024]{1,0:T(8,128)(2,1)S(1)}, u32[]{:S(2)}, u32[]{:S(2)}) %collective-permute-start.2) | collective-permute-done | bytes 65568 | tf_op jit(solution)/shard_map/ppermute | solution.py:16
  114.7 2.5 broadcast_in_dim.50
  117.2 10.9 %while.32 = (s32[]{:T(128)}, bf16[128,16,1024]{2,0,1:T(8,128)(2,1)}, f32[128,16,128]{2,0,1:T(8,128)}, pred[128,16,1024]{0,2,1:T(32,128)(4,1)S(1)}, bf16[128,1024...) while((s32[]{:T(128)}, ...), condition=%wide.region_9.10_spmd.clone, body=%wide.region_8.9_spmd.clone.sunk | while | flops 275316736 | bytes 53494056 | solution.py:115
  117.3 0.1 constant_dynamic-slice_fusion.2
  117.3 1.2 copy.31
  118.6 1.0 fusion.37
  119.6 0.2 copy-done.2
  119.8 0.7 fusion.36
  120.5 0.3 copy-done.5
  120.8 1.9 copy-done.3
  122.7 0.1 constant_dynamic-slice_fusion.2
  122.8 1.2 copy.31
  124.0 1.0 fusion.37
  125.1 0.1 copy-done.2
  125.2 0.7 fusion.36
  125.9 0.3 copy-done.5
  126.2 1.9 copy-done.3
  128.1 4.4 %convolution_bitcast_fusion = f32[1024,128]{1,0:T(8,128)} fusion(bf16[128,16,1024]{2,0,1:T(8,128)(2,1)} %get-tuple-element.285, bf16[128,16,128]{2,1,0:T(8,128)(2,1)S(1)} %copy-done.7), kind=kOutput, calls=%fused_computation.26 | convolution fusion | flops 536870912 | bytes 5242880 | tf_op jit(solution)/shard_map/tjs,tjd->sd/dot_general | solution.py:117
  132.5 1.6 copy.19
  134.1 132.9 %reduce-scatter.5.cloned.1.call-done = f32[32,128]{1,0:T(8,128)} async-done(((f32[1024,128]{1,0:T(8,128)}), f32[32,128]{1,0:T(8,128)}) %reduce-scatter.5.cloned.1.call-update) | async-done | bytes 16400 | tf_op jit(solution)/shard_map/reduce_scatter | solution.py:116
  (48 shorter events, 0.5 us)
Async XLA Ops:
  7.2 31.4 %copy-start.9 = (f32[128,32]{0,1:T(8,128)S(1)}, f32[128,32]{0,1:T(8,128)}, u32[]{:S(2)}) copy-start(f32[128,32]{0,1:T(8,128)} %param.14) | copy-start | bytes 49156
  7.2 29.5 %all-gather.2.cloned.1.call-start = ((), (), s32[]{:S(2)}) async-start(), calls=%async_computation.2 | async-start | bytes 1327104 | tf_op jit(solution)/shard_map/all_gather | solution.py:49
  7.9 85.2 %reduce-scatter.3.cloned.1.call-start = ((), (), s32[]{:S(2)}) async-start(), calls=%async_computation.3 | async-start | bytes 1310720 | tf_op jit(solution)/shard_map/reduce_scatter | solution.py:85
  38.6 27.1 %copy-start.10 = (s32[16]{0:T(128)S(1)}, s32[16]{0:T(128)}, u32[]{:S(2)}) copy-start(s32[16]{0:T(128)} %param.11) | copy-start | bytes 196
  38.6 58.0 %copy-start.8 = (bf16[128,16]{0,1:T(8,128)(2,1)S(1)}, bf16[128,16]{0,1:T(8,128)(2,1)}, u32[]{:S(2)}) copy-start(bf16[128,16]{0,1:T(8,128)(2,1)} %param.17) | copy-start | bytes 12292
  38.6 6.8 %copy-start = (bf16[128,16,128]{2,0,1:T(8,128)(2,1)}, bf16[128,16,128]{2,0,1:T(8,128)(2,1)S(1)}, u32[]{:S(2)}) copy-start(bf16[128,16,128]{2,0,1:T(8,128)(2,1)S(1)} %get-tuple-element.520) | copy-start | bytes 1572868 | tf_op jit(solution)/shard_map/while
  48.4 3.7 %copy-start.1 = (bf16[128,16,128]{2,0,1:T(8,128)(2,1)S(1)}, bf16[128,16,128]{2,0,1:T(8,128)(2,1)}, u32[]{:S(2)}) copy-start(bf16[128,16,128]{2,0,1:T(8,128)(2,1)} %copy-done) | copy-start | bytes 1572868 | tf_op jit(solution)/shard_map/while
  52.1 6.8 %copy-start = (bf16[128,16,128]{2,0,1:T(8,128)(2,1)}, bf16[128,16,128]{2,0,1:T(8,128)(2,1)S(1)}, u32[]{:S(2)}) copy-start(bf16[128,16,128]{2,0,1:T(8,128)(2,1)S(1)} %get-tuple-element.520) | copy-start | bytes 1572868 | tf_op jit(solution)/shard_map/while
  61.9 3.7 %copy-start.1 = (bf16[128,16,128]{2,0,1:T(8,128)(2,1)S(1)}, bf16[128,16,128]{2,0,1:T(8,128)(2,1)}, u32[]{:S(2)}) copy-start(bf16[128,16,128]{2,0,1:T(8,128)(2,1)} %copy-done) | copy-start | bytes 1572868 | tf_op jit(solution)/shard_map/while
  65.6 201.4 %reduce-scatter.5.cloned.1.call-start = ((), (), s32[]{:S(2)}) async-start(), calls=%async_computation.4 | async-start | bytes 540672 | tf_op jit(solution)/shard_map/reduce_scatter | solution.py:116
  96.5 6.1 %collective-permute-start = (bf16[32,1024]{1,0:T(8,128)(2,1)S(1)}, bf16[32,1024]{1,0:T(8,128)(2,1)S(1)}, u32[]{:S(2)}, u32[]{:S(2)}) collective-permute-start(bf16[32,1024]{1,0:T(8,128)(2,1)S(1)} %get-tuple-element.381), channel_id=1, source_target_pairs={{0,1},{1,2},{2,3},{3,0},{4,5},{5,6},{6,7},{7,4},{8,9},{9,10},{10,1... | collective-permute-start | bytes 196616 | tf_op jit(solution)/shard_map/ppermute | solution.py:16
  102.6 6.1 %collective-permute-start.1 = (bf16[32,1024]{1,0:T(8,128)(2,1)S(1)}, bf16[32,1024]{1,0:T(8,128)(2,1)S(1)}, u32[]{:S(2)}, u32[]{:S(2)}) collective-permute-start(bf16[32,1024]{1,0:T(8,128)(2,1)S(1)} %collective-permute-done), channel_id=1, source_target_pairs={{0,1},{1,2},{2,3},{3,0},{4,5},{5,6},{6,7},{7,4},{8,9},{9,10},{10,1... | collective-permute-start | bytes 196616 | tf_op jit(solution)/shard_map/ppermute | solution.py:16
  108.7 6.1 %collective-permute-start.2 = (bf16[32,1024]{1,0:T(8,128)(2,1)S(1)}, bf16[32,1024]{1,0:T(8,128)(2,1)S(1)}, u32[]{:S(2)}, u32[]{:S(2)}) collective-permute-start(bf16[32,1024]{1,0:T(8,128)(2,1)S(1)} %collective-permute-done.1), channel_id=1, source_target_pairs={{0,1},{1,2},{2,3},{3,0},{4,5},{5,6},{6,7},{7,4},{8,9},{9,10},{10,1... | collective-permute-start | bytes 196616 | tf_op jit(solution)/shard_map/ppermute | solution.py:16
  117.2 10.9 %copy-start.7 = (bf16[128,16,128]{2,1,0:T(8,128)(2,1)S(1)}, bf16[128,16,128]{2,1,0:T(8,128)(2,1)}, u32[]{:S(2)}) copy-start(bf16[128,16,128]{2,1,0:T(8,128)(2,1)} %param.15) | copy-start | bytes 1572868
  117.2 1.3 copy-start.4
  117.2 2.5 copy-start.2
  119.8 1.0 copy-start.5
  120.8 1.9 copy-start.3
  122.7 1.3 copy-start.4
  122.7 2.5 copy-start.2
  125.2 1.0 copy-start.5
  126.2 1.9 copy-start.3
  128.1 4.4 %copy-start.6 = (f32[128,16,128]{2,0,1:T(8,128)S(1)}, f32[128,16,128]{2,0,1:T(8,128)}, u32[]{:S(2)}) copy-start(f32[128,16,128]{2,0,1:T(8,128)} %get-tuple-element.344) | copy-start | bytes 3145732
Sparse Core Ops, SparseCore 0:
  9.9 26.7 all-gather.1
  65.8 27.2 reduce-scatter.2
  132.6 134.3 reduce-scatter.4
